TPU v7x, 32 devices: a whole 2x2x4 slice. The times are simulated.
32 devices in a mesh: dp: 8 (over y, x, core), mp: 4 (over z).
Axes of the slice: x: 2, y: 2, z: 4, core: 2. Of those that a mesh axis runs over, the one named last changes fastest.
Arguments:
- activations: bfloat16 [1024, 2560], P('dp'), may hold values from -6 to 6
- grad_hidden: bfloat16 [1024, 8192], P('dp', 'mp'), may hold values from -0.059814453 to 0.059814453
- up_weight: bfloat16 [2560, 8192], P('dp', 'mp'), may hold values from -6 to 6
- error_feedback: bfloat16 [8, 2560, 8192], P('dp', None, 'mp'), may hold values from -0.75 to 0.75
- query_previous: float32 [8192, 128], P('mp'), may hold values from -6 to 6
Outputs:
- grad_input: bfloat16 [1024, 2560], P('dp', 'mp')
- error_next: bfloat16 [8, 2560, 8192], P('dp', None, 'mp')
- update: float32 [2560, 8192], P('dp', 'mp')
- query_next: float32 [8192, 128], P('mp')
All inputs are finite; a program needn't handle non-finite values.
Results may differ from a plain program's by a relative error of at most 0.0005.
Values may be sent and summed in bfloat16 or wider, within the bound.
A program may use at most 128 MiB of HBM per device.

v0:
```python
import jax
import jax.numpy as jnp
from jax import lax
from jax.sharding import PartitionSpec as P

HIGHEST = lax.Precision.HIGHEST


def orthonormal(project, gram_matrix):
    factor = jnp.linalg.cholesky(gram_matrix)
    return lax.linalg.triangular_solve(
        factor, project, left_side=False, lower=True, transpose_a=True
    )


def local(activations, grad_hidden, up_weight, error_feedback, query_previous):
    replicas = lax.axis_size("dp")
    partial_input = lax.dot_general(
        grad_hidden,
        lax.all_gather(up_weight, "dp", axis=0, tiled=True),
        (((1,), (1,)), ((), ())),
        preferred_element_type=jnp.float32,
    )
    grad_input = lax.psum_scatter(partial_input, "mp", scatter_dimension=1, tiled=True).astype(
        jnp.bfloat16
    )
    local_grad = lax.dot_general(
        activations, grad_hidden, (((0,), (0,)), ((), ())), preferred_element_type=jnp.float32
    )
    merged = error_feedback[0].astype(jnp.float32) + local_grad
    project = jnp.dot(merged, query_previous, precision=HIGHEST, preferred_element_type=jnp.float32)
    project = lax.psum(project, ("dp", "mp"))
    gram_matrix = jnp.dot(project.T, project, precision=HIGHEST, preferred_element_type=jnp.float32)
    basis_full = orthonormal(project, gram_matrix)
    query_term = lax.dot_general(
        merged,
        basis_full,
        (((0,), (0,)), ((), ())),
        precision=HIGHEST,
        preferred_element_type=jnp.float32,
    )
    query_next = lax.psum(query_term, "dp") / replicas
    low_rank = lax.dot_general(
        basis_full,
        query_next,
        (((1,), (1,)), ((), ())),
        precision=HIGHEST,
        preferred_element_type=jnp.float32,
    )
    error_next = (merged - low_rank).astype(jnp.bfloat16)[None]
    row_share = merged.shape[0] // replicas
    update = lax.dynamic_slice_in_dim(low_rank, lax.axis_index("dp") * row_share, row_share, 0)
    return (grad_input, error_next, update, query_next)


def solution(mesh):
    in_specs = (P("dp", None), P("dp", "mp"), P("dp", "mp"), P("dp", None, "mp"), P("mp", None))
    out_specs = (P("dp", "mp"), P("dp", None, "mp"), P("dp", "mp"), P("mp", None))
    return jax.shard_map(local, mesh=mesh, in_specs=in_specs, out_specs=out_specs, check_vma=False)
```

profile of v0, /device:TPU:0, one launch (start us, length us, event | category | flops | bytes accessed | tf_op | source)
XLA Modules:
  0.0 408.8 jit_solution(13661397376789167608)
XLA Ops:
  7.2 7.3 %convert_add_fusion = f32[2560,2048]{1,0:T(8,128)S(1)} fusion(bf16[128,2560]{1,0:T(8,128)(2,1)} %param.5, bf16[128,2048]{1,0:T(8,128)(2,1)} %param.6, bf16[1,2560,2048]{2,1,0:T(8,128)(2,1)} %param.8), kind=kOutput, calls=%fused_computation | convolution fusion | flops 1352663040 | bytes 32636928 | tf_op jit(solution)/shard_map/dot_general | solution.py:27
  14.6 7.0 %copy-done.2 = f32[2560,2048]{1,0:T(8,128)} copy-done((f32[2560,2048]{1,0:T(8,128)}, f32[2560,2048]{1,0:T(8,128)S(1)}, u32[]{:S(2)}) %copy-start.2) | copy-done | bytes 20971544
  21.5 17.5 %fusion.6 = f32[2560,128]{1,0:T(8,128)} fusion(f32[2560,2048]{1,0:T(8,128)S(1)} %convert_add_fusion, f32[2048,128]{1,0:T(8,128)S(1)} %copy-done), kind=kOutput, calls=%fused_computation.16 | convolution fusion | flops 8053063680 | bytes 23330816 | tf_op jit(solution)/shard_map/dot_general | solution.py:31
  39.1 0.2 all-reduce.5.cloned.1.call-start
  39.3 134.7 %all-reduce.3.cloned.1.call-done = f32[2560,128]{1,0:T(8,128)} async-done(((f32[2560,128]{1,0:T(8,128)}), f32[2560,128]{1,0:T(8,128)}) %all-reduce.3.cloned.1.call-update) | async-done | bytes 1310736 | tf_op jit(solution)/shard_map/psum | solution.py:32
  174.0 3.9 fusion.7
  177.9 0.1 copy.9
  178.1 11.7 %cholesky.16 = f32[128,128]{1,0:T(8,128)S(1)} custom-call(f32[128,128]{1,0:T(8,128)S(1)} %fusion.4), custom_call_target="Cholesky" | custom-call | tf_op jit(solution)/shard_map/jit(cholesky)/cholesky | solution.py:10
  189.8 0.6 compare_reduce_fusion
  190.5 0.7 fusion.1
  191.1 9.8 %custom-call.6 = f32[1,128,128]{1,2,0:T(8,128)S(1)} custom-call(f32[1,128,128]{2,1,0:T(8,128)S(1)} %fusion.1), custom_call_target="InvertDiagBlocksLowerTriangular" | custom-call | tf_op jit(solution)/shard_map/triangular_solve | solution.py:11
  200.9 2.5 fusion.2
  203.4 36.5 %fusion.8 = f32[2048,128]{1,0:T(8,128)} fusion(f32[2560,2048]{1,0:T(8,128)} %copy-done.2, f32[2560,128]{1,0:T(8,128)S(1)} %fusion.2), kind=kOutput, calls=%fused_computation.18 | convolution fusion | flops 8053063680 | bytes 23330816 | tf_op jit(solution)/shard_map/dot_general | solution.py:35
  240.0 0.7 all-gather.2.cloned.1.call-update
  240.8 55.0 %all-reduce.5.cloned.1.call-done = f32[2048,128]{1,0:T(8,128)} async-done(((f32[2048,128]{1,0:T(8,128)}), f32[2048,128]{1,0:T(8,128)}) %all-reduce.5.cloned.1.call-update) | async-done | bytes 1048592 | tf_op jit(solution)/shard_map/psum | solution.py:42
  295.8 1.3 broadcast_multiply_fusion
  297.1 17.2 %fusion.9 = f32[2560,2048]{1,0:T(8,128)S(1)} fusion(f32[2560,128]{1,0:T(8,128)S(1)} %fusion.2, f32[2048,128]{1,0:T(8,128)S(1)} %broadcast_multiply_fusion), kind=kOutput, calls=%fused_computation.19 | convolution fusion | flops 8053063680 | bytes 23330816 | tf_op jit(solution)/shard_map/dot_general | solution.py:43
  314.3 7.0 %copy-done.3 = f32[2560,2048]{1,0:T(8,128)} copy-done((f32[2560,2048]{1,0:T(8,128)}, f32[2560,2048]{1,0:T(8,128)S(1)}, u32[]{:S(2)}) %copy-start.3) | copy-done | bytes 20971544
  321.3 1.7 constant_dynamic-slice_fusion
  322.9 37.1 %all-gather.2.cloned.1.call-done = bf16[2560,2048]{1,0:T(8,128)(2,1)} async-done(((bf16[320,2048]{1,0:T(8,128)(2,1)}), bf16[2560,2048]{1,0:T(8,128)(2,1)}) %all-gather.2.cloned.1.call-update) | async-done | bytes 10485776 | tf_op jit(solution)/shard_map/all_gather | solution.py:20
  360.1 8.6 %fusion.5 = f32[128,2560]{1,0:T(8,128)} fusion(bf16[128,2048]{1,0:T(8,128)(2,1)S(1)} %copy-done.5, bf16[2560,2048]{1,0:T(8,128)(2,1)} %all-gather.2.cloned.1.call-done), kind=kOutput, calls=%fused_computation.15 | convolution fusion | flops 1342177280 | bytes 12320768 | tf_op jit(solution)/shard_map/dot_general | solution.py:18
  368.7 18.5 %fusion = bf16[1,2560,2048]{2,1,0:T(8,128)(2,1)} fusion(f32[2560,2048]{1,0:T(8,128)} %copy-done.2, f32[2560,2048]{1,0:T(8,128)} %copy-done.3), kind=kLoop, calls=%fused_computation.2 | loop fusion | flops 10485760 | bytes 52428800 | tf_op jit(solution)/shard_map/broadcast_in_dim | solution.py:50
  387.2 13.0 %reduce-scatter.2.cloned.1.call-done = f32[128,640]{1,0:T(8,128)} async-done(((f32[128,2560]{1,0:T(8,128)}), f32[128,640]{1,0:T(8,128)}) %reduce-scatter.2.cloned.1.call-update) | async-done | bytes 327696 | tf_op jit(solution)/shard_map/reduce_scatter | solution.py:24
  400.2 1.7 convert_element_type.12
  (18 shorter events, 0.3 us)
Async XLA Ops:
  7.2 14.4 %copy-start = (f32[2048,128]{1,0:T(8,128)S(1)}, f32[2048,128]{1,0:T(8,128)}, u32[]{:S(2)}) copy-start(f32[2048,128]{1,0:T(8,128)} %param.9) | copy-start | bytes 3145732
  7.2 166.8 %all-reduce.3.cloned.1.call-start = ((), (), s32[]{:S(2)}) async-start(), calls=%async_computation.3 | async-start | bytes 2621440 | tf_op jit(solution)/shard_map/psum | solution.py:32
  14.6 7.0 %copy-start.2 = (f32[2560,2048]{1,0:T(8,128)}, f32[2560,2048]{1,0:T(8,128)S(1)}, u32[]{:S(2)}) copy-start(f32[2560,2048]{1,0:T(8,128)S(1)} %convert_add_fusion) | copy-start | bytes 62914564
  39.1 256.7 %all-reduce.5.cloned.1.call-start = ((), (), s32[]{:S(2)}) async-start(), calls=%async_computation.4 | async-start | bytes 2097152 | tf_op jit(solution)/shard_map/psum | solution.py:42
  240.0 120.1 %all-gather.2.cloned.1.call-start = ((), (), s32[]{:S(2)}) async-start(), calls=%async_computation.1 | async-start | bytes 11796480 | tf_op jit(solution)/shard_map/all_gather | solution.py:20
  240.7 159.5 %reduce-scatter.2.cloned.1.call-start = ((), (), s32[]{:S(2)}) async-start(), calls=%async_computation.2 | async-start | bytes 1638400 | tf_op jit(solution)/shard_map/reduce_scatter | solution.py:24
  297.1 17.2 %copy-start.4 = (f32[2048,128]{1,0:T(8,128)}, f32[2048,128]{1,0:T(8,128)S(1)}, u32[]{:S(2)}) copy-start(f32[2048,128]{1,0:T(8,128)S(1)} %broadcast_multiply_fusion) | copy-start | bytes 3145732
  297.1 63.0 %copy-start.5 = (bf16[128,2048]{1,0:T(8,128)(2,1)S(1)}, bf16[128,2048]{1,0:T(8,128)(2,1)}, u32[]{:S(2)}) copy-start(bf16[128,2048]{1,0:T(8,128)(2,1)} %param.6) | copy-start | bytes 1572868
  314.3 7.0 %copy-start.3 = (f32[2560,2048]{1,0:T(8,128)}, f32[2560,2048]{1,0:T(8,128)S(1)}, u32[]{:S(2)}) copy-start(f32[2560,2048]{1,0:T(8,128)S(1)} %fusion.9) | copy-start | bytes 62914564
  368.7 33.2 %copy-start.1 = (f32[2048,128]{1,0:T(8,128)S(1)}, f32[2048,128]{1,0:T(8,128)}, u32[]{:S(2)}) copy-start(f32[2048,128]{1,0:T(8,128)} %param.9) | copy-start | bytes 3145732
Sparse Core Ops, SparseCore 0:
  39.2 134.7 all-reduce.2
  240.1 55.6 all-reduce.4
  297.7 62.3 all-gather.1
  368.8 31.3 reduce-scatter.1
where the time goes:
time: 415 us; the launch traced here: 409 us
  waiting for transfers between devices  241 us (58%)
  matrix products  93.6 us (23%)
  other arithmetic  44.3 us (11%)
  local copies, waits for them, and re-layouts  15.7 us (4%)
  between operations  14.3 us (3%)
    psum x1, waiting for transfers between devices, local(): project = lax.psum(project, ('dp', 'mp'))  135 us
    psum x1, waiting for transfers between devices, local(): query_next = lax.psum(query_term, 'dp') / replicas  55 us
    all_gather x1, waiting for transfers between devices, local(): lax.all_gather(up_weight, 'dp', axis=0, tiled=True)  37.1 us
    dot_general x1, matrix products, local(): lax.dot_general(merged, basis_full, (((0,), (0,)), ((), ())), precision=H...  36.5 us
    broadcast_in_dim x1, other arithmetic, local(): error_next = (merged - low_rank).astype(jnp.bfloat16)[None]  18.5 us
    dot_general x1, matrix products, local(): jnp.dot(merged, query_previous, precision=HIGHEST, preferred_element_type...  17.5 us
    dot_general x1, matrix products, local(): lax.dot_general(basis_full, query_next, (((1,), (1,)), ((), ())), precisi...  17.2 us
    unnamed x12, local copies, waits for them, and re-layouts  13.9 us
  transfers between devices with their start and end apart: 4, of which 4 were waited for; matrix products, arithmetic and copies ran while one was open for 9% of the time, Pallas kernels for 0%

commit v1 on v0

v1 whole, which is shorter than its diff:
```python
import functools

import jax
import jax.numpy as jnp
from jax import lax
from jax.experimental import pallas as pl
from jax.experimental.pallas import tpu as pltpu
from jax.sharding import PartitionSpec as P

HIGHEST = lax.Precision.HIGHEST
MESH = pl.DeviceIdType.MESH
F32 = jnp.float32
BF16 = jnp.bfloat16
CORES = 2
PANEL = 16


def split(x):
    high = x.astype(BF16)
    return high, (x - high.astype(F32)).astype(BF16)


def dot(a, b, da=1, db=0, precision=None):
    return lax.dot_general(
        a, b, (((da,), (db,)), ((), ())), precision=precision, preferred_element_type=F32
    )


def halves(x):
    r = x.shape[1] // 2
    return x[:, :r] + x[:, r:]


def inverse_factor(gram, aug):
    r = gram.shape[0]
    rows = lax.broadcasted_iota(jnp.int32, (r, r), 0)
    cols = lax.broadcasted_iota(jnp.int32, (r, r), 1)
    aug[:, :r] = gram
    aug[:, r:] = jnp.where(rows == cols, 1.0, 0.0).astype(F32)
    prow = lax.broadcasted_iota(jnp.int32, (PANEL, 2 * r), 0)
    for start in range(0, r, PANEL):
        panel = aug[start : start + PANEL, :]
        for t in range(PANEL):
            j = start + t
            scale = lax.rsqrt(panel[t : t + 1, j : j + 1])
            row = panel[t : t + 1, :] * scale
            col = panel[:, j : j + 1] * scale
            panel = jnp.where(
                prow == t, row, jnp.where(prow > t, panel - col * row, panel)
            )
        aug[start : start + PANEL, :] = panel
        rest = start + PANEL
        if rest < r:
            change = dot(panel[:, :r], panel, 0, 0, HIGHEST)
            aug[rest:, :] = aug[rest:, :] - change[rest:, :]
    return aug[:, r:]


def compress(
    n_dp, n_mp, e_hbm, a_ref, h_hbm, h_ref, q_ref, qn_ref, b_ref,
    e, q2, p, pt2, aug, acc, zin, zfin, csend, crecv, xsend, xrecv,
    t, tcrecv, txsend, txrecv,
    e_sem, c_s, c_r, x_s, x_r, z_s, z_r, gz_s, gz_r, gx_s, gx_r, gc_s, gc_r,
    tc_s, tc_r, tx_s, tx_r, qx_s, qx_r, qc_s, qc_r,
):
    chips = n_dp // CORES
    me, mp = lax.axis_index("dp"), lax.axis_index("mp")
    chip, core = me // CORES, lax.rem(me, CORES)
    other = 1 - core
    partner = (chip * CORES + other, mp)
    d, rank = p.shape
    ff = t.shape[0]
    pr, tr = d // n_dp, ff // n_dp
    zr = pr // n_mp if pr % (8 * n_mp) == 0 else pr

    def chip_at(r):
        return lax.rem(chip + r, chips)

    def same_core(r):
        return (chip_at(r) * CORES + core, mp)

    def along(r):
        return (me, lax.rem(mp + r, n_mp))

    def rows(i, n):
        return pl.ds(pl.multiple_of(i * n, 8), n)

    def send(src, dst, s, r, to):
        return pltpu.make_async_remote_copy(
            src_ref=src, dst_ref=dst, send_sem=s, recv_sem=r, device_id=to, device_id_type=MESH
        )

    barrier = pltpu.get_barrier_semaphore()
    pl.semaphore_signal(barrier, inc=1, device_id=partner, device_id_type=MESH)
    for r in range(1, chips):
        pl.semaphore_signal(barrier, inc=1, device_id=same_core(r), device_id_type=MESH)
    for r in range(1, n_mp):
        pl.semaphore_signal(barrier, inc=1, device_id=along(r), device_id_type=MESH)

    order = [chip_at(r) * CORES + other for r in range(1, chips)] + [partner[0]]
    order += [chip_at(r) * CORES + core for r in range(1, chips)] + [me]
    loads = []
    for i, block in enumerate(order):
        at = pl.ds(pl.multiple_of(block * pr, 16), pr)
        copy = pltpu.make_async_copy(e_hbm.at[at, :], e.at[at, :], e_sem.at[i])
        copy.start()
        loads.append(copy)
    h_load = pltpu.make_async_copy(h_hbm, e.at[pl.ds(d, h_ref.shape[0]), :], e_sem.at[n_dp])
    h_load.start()

    q_high, q_low = split(q_ref[...])
    q2[:, :rank] = q_high
    q2[:, rank:] = q_low
    hq = halves(dot(h_ref[...], q2[...]))
    hq2 = jnp.concatenate(split(hq), axis=1)
    p[...] = halves(dot(a_ref[...], hq2, 0, 0))

    def project(i):
        loads[i].wait()
        block = order[i]
        at = pl.ds(pl.multiple_of(block * pr, 16), pr)
        return halves(dot(e[at, :], q2[...])) + p[rows(block, pr), :]

    pl.semaphore_wait(barrier, 1 + (chips - 1) + (n_mp - 1))
    core_copies = []
    for i in range(chips):
        csend[i] = project(i)
        copy = send(csend.at[i], crecv.at[i], c_s.at[i], c_r.at[i], partner)
        copy.start()
        core_copies.append(copy)
    x_copies = []
    for i in range(chips):
        value = project(chips + i)
        core_copies[i].wait_recv()
        value = value + crecv[i]
        if i < chips - 1:
            xsend[i] = value
            copy = send(xsend.at[i], xrecv.at[i], x_s.at[i], x_r.at[i], same_core(i + 1))
            copy.start()
            x_copies.append(copy)
        else:
            acc[...] = value
    h_load.wait()
    value = acc[...]
    for i, copy in enumerate(x_copies):
        copy.wait_recv()
        value = value + xrecv[i]
    acc[...] = value

    def part(i):
        return rows(i, zr) if zr < pr else pl.ds(0, pr)

    z_copies = []
    for r in range(1, n_mp):
        copy = send(
            acc.at[part(lax.rem(mp + r, n_mp)), :], zin.at[r - 1], z_s.at[r - 1], z_r.at[r - 1], along(r)
        )
        copy.start()
        z_copies.append(copy)
    value = acc[part(mp), :]
    for i, copy in enumerate(z_copies):
        copy.wait_recv()
        value = value + zin[i]
    mine = pl.ds(pl.multiple_of(me * pr, 8), pr)
    if zr < pr:
        zfin[...] = value
        here = pl.ds(pl.multiple_of(me * pr + mp * zr, 8), zr)
        p[here, :] = value
        gz = []
        for r in range(1, n_mp):
            copy = send(zfin, p.at[here, :], gz_s.at[r - 1], gz_r.at[r - 1], along(r))
            copy.start()
            gz.append(copy)
        for r in range(1, n_mp):
            gz[r - 1].wait_recv()
        z_copies += gz
    else:
        p[mine, :] = value

    def gather(ref, n, x_s, x_r, c_s, c_r, between=None):
        own = pl.ds(pl.multiple_of(me * n, 8), n)
        across, down = [], []
        for r in range(1, chips):
            copy = send(ref.at[own, :], ref.at[own, :], x_s.at[r - 1], x_r.at[r - 1], same_core(r))
            copy.start()
            across.append(copy)
        copy = send(ref.at[own, :], ref.at[own, :], c_s.at[chips - 1], c_r.at[chips - 1], partner)
        copy.start()
        down.append(copy)
        if between is not None:
            between()
        for r in range(1, chips):
            across[r - 1].wait_recv()
            block = lax.rem(chip + chips - r, chips) * CORES + core
            at = pl.ds(pl.multiple_of(block * n, 8), n)
            copy = send(ref.at[at, :], ref.at[at, :], c_s.at[r - 1], c_r.at[r - 1], partner)
            copy.start()
            down.append(copy)
        for copy in down:
            copy.wait_recv()
        return across + down

    started = core_copies + x_copies
    for copy in started:
        copy.wait_send()
    for copy in z_copies:
        copy.wait_send()
    for copy in gather(p, pr, gx_s, gx_r, gc_s, gc_r):
        copy.wait_send()

    pt = p[...].T
    high, low = split(pt)
    pt2[:rank, :d] = high
    pt2[rank:, :d] = low
    ap = dot(pt2[:, :d], a_ref[...], 1, 1)
    high, low = split(ap[:rank] + ap[rank:])
    pt2[:rank, d:] = high
    pt2[rank:, d:] = low
    width = 256

    def term(n, carry):
        at = pl.ds(pl.multiple_of(n * width, width), width)
        both = dot(pt2[...], e[:, at])
        t[at, :] = (both[:rank] + both[rank:]).T
        return carry

    lax.fori_loop(0, ff // width, term, 0)
    t_copies = []
    for i in range(chips):
        block = chip_at(i + 1) * CORES + other
        copy = send(t.at[rows(block, tr), :], tcrecv.at[i], tc_s.at[i], tc_r.at[i], partner)
        copy.start()
        t_copies.append(copy)
    gram = dot(pt, p[...], 1, 0, HIGHEST)
    tx_copies = []
    for i in range(chips):
        t_copies[i].wait_recv()
        value = t[rows(chip_at(i + 1) * CORES + core, tr), :] + tcrecv[i]
        txsend[i] = value
        if i < chips - 1:
            copy = send(txsend.at[i], txrecv.at[i], tx_s.at[i], tx_r.at[i], same_core(i + 1))
            copy.start()
            tx_copies.append(copy)
    inverse = inverse_factor(gram, aug)
    value = txsend[chips - 1]
    for i, copy in enumerate(tx_copies):
        copy.wait_recv()
        value = value + txrecv[i]
    for copy in t_copies + tx_copies:
        copy.wait_send()
    qn_ref[rows(me, tr), :] = dot(value, inverse, 1, 1, HIGHEST) / n_dp

    def basis():
        high, low = split(dot(p[...], aug[:, rank:], 1, 1, HIGHEST))
        b_ref[:, :rank] = high
        b_ref[:, rank:] = low

    for copy in gather(qn_ref, tr, qx_s, qx_r, qc_s, qc_r, basis):
        copy.wait_send()


def residual(n_dp, e_ref, a_ref, h_ref, qn_ref, b_ref, out_ref, up_ref, y):
    tok, rank = h_ref.shape[0], qn_ref.shape[1]
    rows = e_ref.shape[0]
    step = pl.program_id(0)

    @pl.when(step == 0)
    def _():
        high, low = split(-qn_ref[...].T)
        y[:rank] = high
        y[rank : 2 * rank] = high
        y[2 * rank : 3 * rank] = low
        y[3 * rank :] = h_ref[...]
        share = up_ref.shape[0]
        own = b_ref[pl.ds(pl.multiple_of(lax.axis_index("dp") * share, 16), share), :]
        x = jnp.concatenate([own, own[:, :rank]], axis=1)
        up_ref[...] = -dot(x, y[: 3 * rank, :])

    b = b_ref[pl.ds(pl.multiple_of(step * rows, 16), rows), :]
    x = jnp.concatenate([b, b[:, :rank], a_ref[...].T], axis=1)
    out_ref[...] = (e_ref[...].astype(F32) + dot(x, y[...])).astype(BF16)


def local(n_dp, n_mp, activations, grad_hidden, up_weight, error_feedback, query_previous):
    error = error_feedback[0]
    d, ff = error.shape
    tok, rank = activations.shape[0], query_previous.shape[1]
    partial_input = lax.dot_general(
        grad_hidden,
        lax.all_gather(up_weight, "dp", axis=0, tiled=True),
        (((1,), (1,)), ((), ())),
        preferred_element_type=F32,
    )
    grad_input = lax.psum_scatter(partial_input, "mp", scatter_dimension=1, tiled=True).astype(BF16)

    chips = n_dp // CORES
    pr, tr = d // n_dp, ff // n_dp
    zr = pr // n_mp if pr % (8 * n_mp) == 0 else pr
    vmem = pl.BlockSpec(memory_space=pltpu.VMEM)
    hbm = pl.BlockSpec(memory_space=pl.ANY)
    dma = pltpu.SemaphoreType.DMA
    pairs = lambda n: [dma((n,)), dma((n,))]
    query_next, basis = pl.pallas_call(
        functools.partial(compress, n_dp, n_mp),
        out_shape=(
            jax.ShapeDtypeStruct((ff, rank), F32),
            jax.ShapeDtypeStruct((d, 2 * rank), BF16),
        ),
        in_specs=[hbm, vmem, hbm, vmem, vmem],
        out_specs=(vmem, vmem),
        scratch_shapes=[
            pltpu.VMEM((d + tok, ff), BF16),
            pltpu.VMEM((ff, 2 * rank), BF16),
            pltpu.VMEM((d, rank), F32),
            pltpu.VMEM((2 * rank, d + tok), BF16),
            pltpu.VMEM((rank, 2 * rank), F32),
            pltpu.VMEM((pr, rank), F32),
            pltpu.VMEM((n_mp, zr, rank), F32),
            pltpu.VMEM((zr, rank), F32),
            pltpu.VMEM((chips, pr, rank), F32),
            pltpu.VMEM((chips, pr, rank), F32),
            pltpu.VMEM((chips, pr, rank), F32),
            pltpu.VMEM((chips, pr, rank), F32),
            pltpu.VMEM((ff, rank), F32),
            pltpu.VMEM((chips, tr, rank), F32),
            pltpu.VMEM((chips, tr, rank), F32),
            pltpu.VMEM((chips, tr, rank), F32),
            dma((n_dp + 1,)),
        ]
        + pairs(chips) + pairs(chips) + pairs(n_mp) + pairs(n_mp) + pairs(chips) + pairs(chips)
        + pairs(chips) + pairs(chips) + pairs(chips) + pairs(chips),
        compiler_params=pltpu.CompilerParams(
            collective_id=0, has_side_effects=True, vmem_limit_bytes=48 << 20
        ),
        cost_estimate=pl.CostEstimate(flops=8 * d * ff * rank, bytes_accessed=4 * d * ff, transcendentals=0),
        name="compress",
    )(error, activations, grad_hidden, grad_hidden, query_previous)

    block = 256
    error_next, update = pl.pallas_call(
        functools.partial(residual, n_dp),
        out_shape=(
            jax.ShapeDtypeStruct((d, ff), BF16),
            jax.ShapeDtypeStruct((pr, ff), F32),
        ),
        grid=(d // block,),
        in_specs=[
            pl.BlockSpec((block, ff), lambda i: (i, 0)),
            pl.BlockSpec((tok, block), lambda i: (0, i)),
            pl.BlockSpec((tok, ff), lambda i: (0, 0)),
            pl.BlockSpec((ff, rank), lambda i: (0, 0)),
            pl.BlockSpec((d, 2 * rank), lambda i: (0, 0)),
        ],
        out_specs=(
            pl.BlockSpec((block, ff), lambda i: (i, 0)),
            pl.BlockSpec((pr, ff), lambda i: (0, 0)),
        ),
        scratch_shapes=[pltpu.VMEM((3 * rank + tok, ff), BF16)],
        compiler_params=pltpu.CompilerParams(vmem_limit_bytes=40 << 20),
        cost_estimate=pl.CostEstimate(flops=8 * d * ff * rank, bytes_accessed=4 * d * ff, transcendentals=0),
        name="residual",
    )(error, activations, grad_hidden, query_next, basis)
    return grad_input, error_next[None], update, query_next


def solution(mesh):
    n_dp, n_mp = mesh.shape["dp"], mesh.shape["mp"]
    in_specs = (P("dp", None), P("dp", "mp"), P("dp", "mp"), P("dp", None, "mp"), P("mp", None))
    out_specs = (P("dp", "mp"), P("dp", None, "mp"), P("dp", "mp"), P("mp", None))
    return jax.shard_map(
        functools.partial(local, n_dp, n_mp),
        mesh=mesh, in_specs=in_specs, out_specs=out_specs, check_vma=False,
    )
```

time: 415 us -> 184 us (0.44); the launches traced: 409 us -> 183 us
  waiting for transfers between devices: 241 us -> 68.5 us
  Pallas kernels: 0 us -> 85 us
  matrix products: 93.6 us -> 8.81 us
  other arithmetic: 44.3 us -> 1.66 us
  local copies, waits for them, and re-layouts: 15.7 us -> 4.96 us
    psum x2 -> x0, waiting for transfers between devices: 190 us -> none  [the longest x1 135 us: local(): project = lax.psum(project, ('dp', 'mp'))]
    pallas_call x0 -> x2, Pallas kernels: none -> 85 us  [the longest x1 74.5 us: local(): pl.pallas_call(functools.partial(compress, n_dp, n_mp), out_shape=(jax.Sh...]
    dot_general x5 -> x0, matrix products: 82.5 us -> none  [the longest x1 36.5 us: local(): lax.dot_general(merged, basis_full, (((0,), (0,)), ((), ())), precision=H...]
    all_gather x1, waiting for transfers between devices: 37.1 us -> 67.8 us  [local(): lax.all_gather(up_weight, 'dp', axis=0, tiled=True)]
    another operation x5 -> x0, other arithmetic: 22.9 us -> none  [the longest x3 12.4 us: orthonormal(): factor = jnp.linalg.cholesky(gram_matrix)]
    broadcast_in_dim x1 -> x0, other arithmetic: 18.5 us -> none  [local(): error_next = (merged - low_rank).astype(jnp.bfloat16)[None]]
    reduce_scatter x1, waiting for transfers between devices: 13 us -> 0.01 us  [local(): lax.psum_scatter(partial_input, 'mp', scatter_dimension=1, tiled=True)]
    unnamed x12 -> x9, local copies, waits for them, and re-layouts: 13.9 us -> 4.96 us
  transfers between devices with their start and end apart: 4 -> 2, of which waited for: 4 -> 1; matrix products, arithmetic and copies ran while one was open for 9% -> 0% of each run, Pallas kernels for 0% -> 46%
where the time goes in v1:
time: 184 us; the launch traced here: 183 us
  Pallas kernels  85 us (46%)
  waiting for transfers between devices  68.5 us (37%)
  between operations  14.1 us (8%)
  matrix products  8.81 us (5%)
  local copies, waits for them, and re-layouts  4.96 us (3%)
    pallas_call x1, Pallas kernels, local(): pl.pallas_call(functools.partial(compress, n_dp, n_mp), out_shape=(jax.Sh...  74.5 us
    all_gather x1, waiting for transfers between devices, local(): lax.all_gather(up_weight, 'dp', axis=0, tiled=True)  67.8 us
    pallas_call x1, Pallas kernels, local(): pl.pallas_call(functools.partial(residual, n_dp), out_shape=(jax.ShapeDty...  10.5 us
    dot_general x1, matrix products, local(): lax.dot_general(grad_hidden, lax.all_gather(up_weight, 'dp', axis=0, tile...  8.81 us
    unnamed x9, local copies, waits for them, and re-layouts  4.96 us
  transfers between devices with their start and end apart: 2, of which 1 were waited for; matrix products, arithmetic and copies ran while one was open for 0% of the time, Pallas kernels for 46%

profile of v1, /device:TPU:0, one launch (start us, length us, event | category | flops | bytes accessed | tf_op | source)
XLA Modules:
  0.0 183.1 jit_solution(6032228764844855989)
XLA Ops:
  7.2 0.0 copy-start
  7.2 0.0 copy-start.3
  7.2 0.0 copy-start.2
  7.2 0.0 all-gather.2.cloned.1.call-start
  7.2 0.7 all-gather.2.cloned.1.call-update
  7.9 0.0 reduce-scatter.2.cloned.1.call-start
  8.0 67.8 %all-gather.2.cloned.1.call-done = bf16[2560,2048]{1,0:T(8,128)(2,1)} async-done(((bf16[320,2048]{1,0:T(8,128)(2,1)}), bf16[2560,2048]{1,0:T(8,128)(2,1)}) %all-gather.2.cloned.1.call-update) | async-done | bytes 10485776 | tf_op jit(solution)/shard_map/all_gather | solution.py:290
  75.8 8.8 %fusion = f32[128,2560]{1,0:T(8,128)} fusion(bf16[128,2048]{1,0:T(8,128)(2,1)} %h_ref.3, bf16[2560,2048]{1,0:T(8,128)(2,1)} %all-gather.2.cloned.1.call-done), kind=kOutput, calls=%fused_computation | convolution fusion | flops 1342177280 | bytes 12320768 | tf_op jit(solution)/shard_map/dot_general | solution.py:288
  84.6 0.0 reduce-scatter.2.cloned.1.call-update
  84.6 0.0 copy-done
  84.6 0.0 copy-done.3
  84.6 0.0 copy-done.2
  84.6 74.5 %compress.1 = (f32[2048,128]{1,0:T(8,128)S(1)}, bf16[2560,256]{1,0:T(8,128)(2,1)S(1)}) custom-call(bf16[2560,2048]{1,0:T(8,128)(2,1)} %bitcast.4, bf16[128,2560]{1,0:T(8,128)(2,1)S(1)} %copy-done.3, bf16[128,2048]{1,0:T(8,128)(2,1)S(1)} %copy-done, bf16[128,2048]{1,0:T(8,128)(2,1)S(1)} %copy-done, f32[2048,128]{1,0:T(8,128)S(1)} %copy-done.2), custom_call_target="tpu_custom_call" | custom-call | flops 5368709120 | bytes 20971520 | tf_op jit(solution)/shard_map/compress/pallas_call | solution.py:303
  159.1 0.0 copy-start.1
  159.2 4.0 %copy-done.1 = bf16[1,2560,2048]{2,1,0:T(8,128)(2,1)S(1)} copy-done((bf16[1,2560,2048]{2,1,0:T(8,128)(2,1)S(1)}, bf16[1,2560,2048]{2,1,0:T(8,128)(2,1)}, u32[]{:S(2)}) %copy-start.1) | copy-done | bytes 10485784
  163.1 10.5 %residual.1 = (bf16[2560,2048]{1,0:T(8,128)(2,1)}, f32[320,2048]{1,0:T(8,128)}) custom-call(bf16[2560,2048]{1,0:T(8,128)(2,1)S(1)} %bitcast.5, bf16[128,2560]{1,0:T(8,128)(2,1)S(1)} %copy-done.3, bf16[128,2048]{1,0:T(8,128)(2,1)S(1)} %copy-done, f32[2048,128]{1,0:T(8,128)S(1)} %get-tuple-element.19.qn_ref, bf16[2560,256]{1,0:T(8,128)(2,1)S(1)} %get-tuple-element.9.b_ref), custom_call_target="tpu_custom_call" | custom-call | flops 5368709120 | bytes 20971520 | tf_op jit(solution)/shard_map/residual/pallas_call | solution.py:340
  173.6 0.0 reduce-scatter.2.cloned.1.call-done
  173.6 1.7 convert_element_type.3
  175.3 1.0 copy.10
Async XLA Ops:
  7.2 77.4 %copy-start = (bf16[128,2048]{1,0:T(8,128)(2,1)S(1)}, bf16[128,2048]{1,0:T(8,128)(2,1)}, u32[]{:S(2)}) copy-start(bf16[128,2048]{1,0:T(8,128)(2,1)} %h_ref.3) | copy-start | bytes 1572868
  7.2 77.4 %copy-start.3 = (bf16[128,2560]{1,0:T(8,128)(2,1)S(1)}, bf16[128,2560]{1,0:T(8,128)(2,1)}, u32[]{:S(2)}) copy-start(bf16[128,2560]{1,0:T(8,128)(2,1)} %a_ref.3) | copy-start | bytes 1966084
  7.2 77.4 %copy-start.2 = (f32[2048,128]{1,0:T(8,128)S(1)}, f32[2048,128]{1,0:T(8,128)}, u32[]{:S(2)}) copy-start(f32[2048,128]{1,0:T(8,128)} %q_ref.1) | copy-start | bytes 3145732
  7.2 68.6 %all-gather.2.cloned.1.call-start = ((), (), s32[]{:S(2)}) async-start(), calls=%async_computation.1 | async-start | bytes 11796480 | tf_op jit(solution)/shard_map/all_gather | solution.py:290
  7.9 165.7 %reduce-scatter.2.cloned.1.call-start = ((), (), s32[]{:S(2)}) async-start(), calls=%async_computation.2 | async-start | bytes 1638400 | tf_op jit(solution)/shard_map/reduce_scatter | solution.py:294
  159.1 4.0 %copy-start.1 = (bf16[1,2560,2048]{2,1,0:T(8,128)(2,1)S(1)}, bf16[1,2560,2048]{2,1,0:T(8,128)(2,1)}, u32[]{:S(2)}) copy-start(bf16[1,2560,2048]{2,1,0:T(8,128)(2,1)} %param.8) | copy-start | bytes 31457284
Sparse Core Ops, SparseCore 0:
  9.9 65.8 all-gather.1
  84.7 36.6 reduce-scatter.1

commit v2 on v1

--- a/solution.py
+++ b/solution.py
@@ -57,11 +57,12 @@
 
 
 def compress(
-    n_dp, n_mp, e_hbm, a_ref, h_hbm, h_ref, q_ref, qn_ref, b_ref,
+    n_dp, n_mp, e_hbm, a_ref, h_hbm, h_ref, q_ref, w_ref, qn_ref, b_ref, gi_ref,
     e, q2, p, pt2, aug, acc, zin, zfin, csend, crecv, xsend, xrecv,
-    t, tcrecv, txsend, txrecv,
+    t, tcrecv, txsend, txrecv, hall, gsend, grecv,
     e_sem, c_s, c_r, x_s, x_r, z_s, z_r, gz_s, gz_r, gx_s, gx_r, gc_s, gc_r,
     tc_s, tc_r, tx_s, tx_r, qx_s, qx_r, qc_s, qc_r,
+    hx_s, hx_r, hc_s, hc_r, g_s, g_r,
 ):
     chips = n_dp // CORES
     me, mp = lax.axis_index("dp"), lax.axis_index("mp")
@@ -97,6 +98,16 @@
     for r in range(1, n_mp):
         pl.semaphore_signal(barrier, inc=1, device_id=along(r), device_id_type=MESH)
 
+    group = n_dp // n_mp
+    target = me // group
+    for k in range(group):
+        for m in range(n_mp):
+            source = mp * group + k
+
+            @pl.when(jnp.logical_or(source != me, mp != m))
+            def _(source=source, m=m):
+                pl.semaphore_signal(barrier, inc=1, device_id=(source, m), device_id_type=MESH)
+
     order = [chip_at(r) * CORES + other for r in range(1, chips)] + [partner[0]]
     order += [chip_at(r) * CORES + core for r in range(1, chips)] + [me]
     loads = []
@@ -121,7 +132,7 @@
         at = pl.ds(pl.multiple_of(block * pr, 16), pr)
         return halves(dot(e[at, :], q2[...])) + p[rows(block, pr), :]
 
-    pl.semaphore_wait(barrier, 1 + (chips - 1) + (n_mp - 1))
+    pl.semaphore_wait(barrier, chips + n_mp - 1 + n_dp - jnp.where(target == mp, 1, 0))
     core_copies = []
     for i in range(chips):
         csend[i] = project(i)
@@ -140,6 +151,27 @@
             x_copies.append(copy)
         else:
             acc[...] = value
+    h_across = [
+        send(h_ref, hall.at[me], hx_s.at[r - 1], hx_r.at[r - 1], same_core(r)) for r in range(1, chips)
+    ]
+    early = min(2, chips - 1)
+    for copy in h_across[:early]:
+        copy.start()
+    h_down = [send(h_ref, hall.at[me], hc_s.at[chips - 1], hc_r.at[chips - 1], partner)]
+    h_down[0].start()
+
+    def late_sends():
+        for copy in h_across[early:]:
+            copy.start()
+
+    def pass_down(rs):
+        for r in rs:
+            h_across[r - 1].wait_recv()
+            block = lax.rem(chip + chips - r, chips) * CORES + core
+            copy = send(hall.at[block], hall.at[block], hc_s.at[r - 1], hc_r.at[r - 1], partner)
+            copy.start()
+            h_down.append(copy)
+
     h_load.wait()
     value = acc[...]
     for i, copy in enumerate(x_copies):
@@ -205,8 +237,9 @@
         copy.wait_send()
     for copy in z_copies:
         copy.wait_send()
-    for copy in gather(p, pr, gx_s, gx_r, gc_s, gc_r):
-        copy.wait_send()
+    for copy in gather(p, pr, gx_s, gx_r, gc_s, gc_r, late_sends):
+        copy.wait_send()
+    pass_down(range(1, early + 1))
 
     pt = p[...].T
     high, low = split(pt)
@@ -241,6 +274,33 @@
             copy = send(txsend.at[i], txrecv.at[i], tx_s.at[i], tx_r.at[i], same_core(i + 1))
             copy.start()
             tx_copies.append(copy)
+    pass_down(range(early + 1, chips))
+    for copy in h_down:
+        copy.wait_recv()
+
+    slot = lax.rem(me, group) * n_mp + mp
+
+    def outgoing(i):
+        to = (lax.rem(me + i, n_dp), target)
+        return send(gsend.at[i], grecv.at[slot], g_s.at[i], g_r.at[slot], to)
+
+    def partial(i, carry):
+        gsend[i] = dot(hall[lax.rem(me + i, n_dp)], w_ref[...], 1, 1)
+        outgoing(i).start()
+        return carry
+
+    lax.fori_loop(1, n_dp, partial, 0)
+    own_part = dot(h_ref[...], w_ref[...], 1, 1)
+
+    @pl.when(target == mp)
+    def _():
+        grecv[slot] = own_part
+
+    @pl.when(target != mp)
+    def _():
+        gsend[0] = own_part
+        outgoing(0).start()
+
     inverse = inverse_factor(gram, aug)
     value = txsend[chips - 1]
     for i, copy in enumerate(tx_copies):
@@ -256,6 +316,27 @@
         b_ref[:, rank:] = low
 
     for copy in gather(qn_ref, tr, qx_s, qx_r, qc_s, qc_r, basis):
+        copy.wait_send()
+    for k in range(group):
+        for m in range(n_mp):
+            i = k * n_mp + m
+
+            @pl.when(jnp.logical_or(mp * group + k != me, mp != m))
+            def _(i=i):
+                send(gsend.at[i], grecv.at[i], g_s.at[i], g_r.at[i], partner).wait_recv()
+
+        total = grecv[k * n_mp]
+        for m in range(1, n_mp):
+            total = total + grecv[k * n_mp + m]
+        gi_ref[k] = total.astype(BF16)
+    for i in range(1, n_dp):
+        outgoing(i).wait_send()
+
+    @pl.when(target != mp)
+    def _():
+        outgoing(0).wait_send()
+
+    for copy in h_across + h_down:
         copy.wait_send()
 
 
@@ -285,14 +366,6 @@
     error = error_feedback[0]
     d, ff = error.shape
     tok, rank = activations.shape[0], query_previous.shape[1]
-    partial_input = lax.dot_general(
-        grad_hidden,
-        lax.all_gather(up_weight, "dp", axis=0, tiled=True),
-        (((1,), (1,)), ((), ())),
-        preferred_element_type=F32,
-    )
-    grad_input = lax.psum_scatter(partial_input, "mp", scatter_dimension=1, tiled=True).astype(BF16)
-
     chips = n_dp // CORES
     pr, tr = d // n_dp, ff // n_dp
     zr = pr // n_mp if pr % (8 * n_mp) == 0 else pr
@@ -300,14 +373,15 @@
     hbm = pl.BlockSpec(memory_space=pl.ANY)
     dma = pltpu.SemaphoreType.DMA
     pairs = lambda n: [dma((n,)), dma((n,))]
-    query_next, basis = pl.pallas_call(
+    query_next, basis, input_blocks = pl.pallas_call(
         functools.partial(compress, n_dp, n_mp),
         out_shape=(
             jax.ShapeDtypeStruct((ff, rank), F32),
             jax.ShapeDtypeStruct((d, 2 * rank), BF16),
+            jax.ShapeDtypeStruct((n_dp // n_mp, tok, pr), BF16),
         ),
-        in_specs=[hbm, vmem, hbm, vmem, vmem],
-        out_specs=(vmem, vmem),
+        in_specs=[hbm, vmem, hbm, vmem, vmem, vmem],
+        out_specs=(vmem, vmem, vmem),
         scratch_shapes=[
             pltpu.VMEM((d + tok, ff), BF16),
             pltpu.VMEM((ff, 2 * rank), BF16),
@@ -325,16 +399,20 @@
             pltpu.VMEM((chips, tr, rank), F32),
             pltpu.VMEM((chips, tr, rank), F32),
             pltpu.VMEM((chips, tr, rank), F32),
+            pltpu.VMEM((n_dp, tok, ff), BF16),
+            pltpu.VMEM((n_dp, tok, pr), F32),
+            pltpu.VMEM((n_dp, tok, pr), F32),
             dma((n_dp + 1,)),
         ]
         + pairs(chips) + pairs(chips) + pairs(n_mp) + pairs(n_mp) + pairs(chips) + pairs(chips)
-        + pairs(chips) + pairs(chips) + pairs(chips) + pairs(chips),
+        + pairs(chips) + pairs(chips) + pairs(chips) + pairs(chips) + pairs(chips) + pairs(chips) + pairs(n_dp),
         compiler_params=pltpu.CompilerParams(
             collective_id=0, has_side_effects=True, vmem_limit_bytes=48 << 20
         ),
         cost_estimate=pl.CostEstimate(flops=8 * d * ff * rank, bytes_accessed=4 * d * ff, transcendentals=0),
         name="compress",
-    )(error, activations, grad_hidden, grad_hidden, query_previous)
+    )(error, activations, grad_hidden, grad_hidden, query_previous, up_weight)
+    grad_input = jnp.swapaxes(input_blocks, 0, 1).reshape(tok, d // n_mp)
 
     block = 256
     error_next, update = pl.pallas_call(

time: 184 us -> 189 us (1.027)
  Pallas kernels: 85 us -> 175 us
  waiting for transfers between devices: 68.5 us -> 0 us
  between operations: 14.1 us -> 0.67 us
  matrix products: 8.81 us -> 0 us
  local copies, waits for them, and re-layouts: 4.96 us -> 13 us
    pallas_call x1, Pallas kernels: 74.5 us -> 164 us  [local(): pl.pallas_call(functools.partial(compress, n_dp, n_mp), out_shape=(jax.Sh...]
    all_gather x1 -> x0, waiting for transfers between devices: 67.8 us -> none  [local(): lax.all_gather(up_weight, 'dp', axis=0, tiled=True)]
    dot_general x1 -> x0, matrix products: 8.81 us -> none  [local(): lax.dot_general(grad_hidden, lax.all_gather(up_weight, 'dp', axis=0, tile...]
    unnamed x9 -> x20, local copies, waits for them, and re-layouts: 4.96 us -> 12.8 us
  transfers between devices with their start and end apart: 2 -> 0, of which waited for: 1 -> 0; matrix products, arithmetic and copies ran while one was open for 0% -> 0% of each run, Pallas kernels for 46% -> 0%
where the time goes in v2:
time: 189 us; the launch traced here: 188 us
  Pallas kernels  175 us (93%)
  local copies, waits for them, and re-layouts  13 us (7%)
    pallas_call x1, Pallas kernels, local(): pl.pallas_call(functools.partial(compress, n_dp, n_mp), out_shape=(jax.Sh...  164 us
    unnamed x20, local copies, waits for them, and re-layouts  12.8 us
    pallas_call x1, Pallas kernels, local(): pl.pallas_call(functools.partial(residual, n_dp), out_shape=(jax.ShapeDty...  10.5 us

profile of v2, /device:TPU:0, one launch (start us, length us, event | category | flops | bytes accessed | tf_op | source)
XLA Modules:
  0.0 188.3 jit_solution(7088882918165638227)
XLA Ops:
  0.6 0.0 copy-start.1
  0.6 1.3 copy-done.1
  1.9 0.0 copy-start.2
  2.0 1.2 copy-done.2
  3.2 0.0 copy-start.3
  3.2 1.1 copy-done.3
  4.3 0.0 copy-start.5
  4.3 1.0 copy-done.5
  5.3 0.0 copy-start.4
  5.3 0.0 copy-start.6
  5.3 164.2 %compress.1 = (f32[2048,128]{1,0:T(8,128)S(1)}, bf16[2560,256]{1,0:T(8,128)(2,1)S(1)}, bf16[2,128,320]{2,1,0:T(8,128)(2,1)S(1)}) custom-call(bf16[2560,2048]{1,0:T(8,128)(2,1)} %bitcast.5, bf16[128,2560]{1,0:T(8,128)(2,1)S(1)} %copy-done.3, bf16[128,2048]{1,0:T(8,128)(2,1)S(1)} %copy-done.5, bf16[128,2048]{1,0:T(8,128)(2,1)S(1)} %copy-done.5, ...), custom_call_target="tpu_custom_call" | custom-call | flops 5368709120 | bytes 20971520 | tf_op jit(solution)/shard_map/compress/pallas_call | solution.py:376
  169.5 0.0 copy-start.7
  169.5 1.0 copy-done.7
  170.5 0.2 copy.9
  170.7 0.8 copy.10
  171.5 0.0 copy-done.4
  171.5 0.0 copy-done.6
  171.5 0.0 copy-start
  171.5 4.0 %copy-done = bf16[1,2560,2048]{2,1,0:T(8,128)(2,1)S(1)} copy-done((bf16[1,2560,2048]{2,1,0:T(8,128)(2,1)S(1)}, bf16[1,2560,2048]{2,1,0:T(8,128)(2,1)}, u32[]{:S(2)}) %copy-start) | copy-done | bytes 10485784
  175.5 0.0 copy-start.8
  175.5 1.3 copy-done.8
  176.8 10.5 %residual.1 = (bf16[2560,2048]{1,0:T(8,128)(2,1)}, f32[320,2048]{1,0:T(8,128)}) custom-call(bf16[2560,2048]{1,0:T(8,128)(2,1)S(1)} %bitcast.6, bf16[128,2560]{1,0:T(8,128)(2,1)S(1)} %copy-done.4, bf16[128,2048]{1,0:T(8,128)(2,1)S(1)} %copy-done.6, f32[2048,128]{1,0:T(8,128)S(1)} %get-tuple-element.25.qn_ref, bf16[2560,256]{1,0:T(8,128)(2,1)S(1)} %copy-done.8), custom_call_target="tpu_custom_call" | custom-call | flops 5368709120 | bytes 20971520 | tf_op jit(solution)/shard_map/residual/pallas_call | solution.py:418
  187.3 1.0 copy.12
Async XLA Ops:
  0.6 1.3 copy-start.1
  1.9 1.2 copy-start.2
  3.2 1.1 copy-start.3
  4.3 1.0 copy-start.5
  5.3 166.2 %copy-start.4 = (bf16[128,2560]{1,0:T(8,128)(2,1)S(1)}, bf16[128,2560]{1,0:T(8,128)(2,1)}, u32[]{:S(2)}) copy-start(bf16[128,2560]{1,0:T(8,128)(2,1)} %a_ref.3) | copy-start | bytes 1966084
  5.3 166.2 %copy-start.6 = (bf16[128,2048]{1,0:T(8,128)(2,1)S(1)}, bf16[128,2048]{1,0:T(8,128)(2,1)}, u32[]{:S(2)}) copy-start(bf16[128,2048]{1,0:T(8,128)(2,1)} %h_ref.3) | copy-start | bytes 1572868
  169.5 1.1 copy-start.7
  171.5 4.0 %copy-start = (bf16[1,2560,2048]{2,1,0:T(8,128)(2,1)S(1)}, bf16[1,2560,2048]{2,1,0:T(8,128)(2,1)}, u32[]{:S(2)}) copy-start(bf16[1,2560,2048]{2,1,0:T(8,128)(2,1)} %param.8) | copy-start | bytes 31457284
  175.5 1.3 copy-start.8

commit v3 on v1

--- a/solution.py
+++ b/solution.py
@@ -57,7 +57,7 @@
 
 
 def compress(
-    n_dp, n_mp, e_hbm, a_ref, h_hbm, h_ref, q_ref, qn_ref, b_ref,
+    n_dp, n_mp, e_hbm, a_ref, h_hbm, h_ref, q_ref, qn_ref, b_ref, h_out,
     e, q2, p, pt2, aug, acc, zin, zfin, csend, crecv, xsend, xrecv,
     t, tcrecv, txsend, txrecv,
     e_sem, c_s, c_r, x_s, x_r, z_s, z_r, gz_s, gz_r, gx_s, gx_r, gc_s, gc_r,
@@ -108,6 +108,7 @@
     h_load = pltpu.make_async_copy(h_hbm, e.at[pl.ds(d, h_ref.shape[0]), :], e_sem.at[n_dp])
     h_load.start()
 
+    h_out[...] = h_ref[...]
     q_high, q_low = split(q_ref[...])
     q2[:, :rank] = q_high
     q2[:, rank:] = q_low
@@ -285,14 +286,7 @@
     error = error_feedback[0]
     d, ff = error.shape
     tok, rank = activations.shape[0], query_previous.shape[1]
-    partial_input = lax.dot_general(
-        grad_hidden,
-        lax.all_gather(up_weight, "dp", axis=0, tiled=True),
-        (((1,), (1,)), ((), ())),
-        preferred_element_type=F32,
-    )
-    grad_input = lax.psum_scatter(partial_input, "mp", scatter_dimension=1, tiled=True).astype(BF16)
-
+    weight = lax.all_gather(up_weight, "dp", axis=0, tiled=True)
     chips = n_dp // CORES
     pr, tr = d // n_dp, ff // n_dp
     zr = pr // n_mp if pr % (8 * n_mp) == 0 else pr
@@ -300,14 +294,15 @@
     hbm = pl.BlockSpec(memory_space=pl.ANY)
     dma = pltpu.SemaphoreType.DMA
     pairs = lambda n: [dma((n,)), dma((n,))]
-    query_next, basis = pl.pallas_call(
+    query_next, basis, hidden = pl.pallas_call(
         functools.partial(compress, n_dp, n_mp),
         out_shape=(
             jax.ShapeDtypeStruct((ff, rank), F32),
             jax.ShapeDtypeStruct((d, 2 * rank), BF16),
+            jax.ShapeDtypeStruct((tok, ff), BF16),
         ),
         in_specs=[hbm, vmem, hbm, vmem, vmem],
-        out_specs=(vmem, vmem),
+        out_specs=(vmem, vmem, vmem),
         scratch_shapes=[
             pltpu.VMEM((d + tok, ff), BF16),
             pltpu.VMEM((ff, 2 * rank), BF16),
@@ -332,9 +327,11 @@
         compiler_params=pltpu.CompilerParams(
             collective_id=0, has_side_effects=True, vmem_limit_bytes=48 << 20
         ),
-        cost_estimate=pl.CostEstimate(flops=8 * d * ff * rank, bytes_accessed=4 * d * ff, transcendentals=0),
+        cost_estimate=pl.CostEstimate(flops=64 * d * ff * rank, bytes_accessed=48 * d * ff, transcendentals=0),
         name="compress",
     )(error, activations, grad_hidden, grad_hidden, query_previous)
+    partial_input = dot(hidden, weight, 1, 1)
+    grad_input = lax.psum_scatter(partial_input, "mp", scatter_dimension=1, tiled=True).astype(BF16)
 
     block = 256
     error_next, update = pl.pallas_call(

time: 184 us -> 142 us (0.77)
  waiting for transfers between devices: 68.5 us -> 15.6 us
  Pallas kernels: 85 us -> 90.9 us
  local copies, waits for them, and re-layouts: 4.96 us -> 10.8 us
    all_gather x1, waiting for transfers between devices: 67.8 us -> 0.29 us  [local(): weight = lax.all_gather(up_weight, 'dp', axis=0, tiled=True)]
    reduce_scatter x1, waiting for transfers between devices: 0.01 us -> 14.6 us  [local(): lax.psum_scatter(partial_input, 'mp', scatter_dimension=1, tiled=True)]
    pallas_call x1, Pallas kernels: 74.5 us -> 80.4 us  [local(): pl.pallas_call(functools.partial(compress, n_dp, n_mp), out_shape=(jax.Sh...]
    unnamed x9 -> x17, local copies, waits for them, and re-layouts: 4.96 us -> 10.8 us
  transfers between devices with their start and end apart: 2 -> 2, of which waited for: 1 -> 2; matrix products, arithmetic and copies ran while one was open for 0% -> 0% of each run, Pallas kernels for 46% -> 64%
where the time goes in v3:
time: 142 us
  Pallas kernels  90.9 us (64%)
  waiting for transfers between devices  15.6 us (11%)
  between operations  14.1 us (10%)
  local copies, waits for them, and re-layouts  10.8 us (8%)
  matrix products  8.66 us (6%)
  other arithmetic  1.66 us (1%)
    pallas_call x1, Pallas kernels, local(): pl.pallas_call(functools.partial(compress, n_dp, n_mp), out_shape=(jax.Sh...  80.4 us
    reduce_scatter x1, waiting for transfers between devices, local(): lax.psum_scatter(partial_input, 'mp', scatter_dimension=1, tiled=True)  14.6 us
    unnamed x17, local copies, waits for them, and re-layouts  10.8 us
    pallas_call x1, Pallas kernels, local(): pl.pallas_call(functools.partial(residual, n_dp), out_shape=(jax.ShapeDty...  10.5 us
    dot_general x1, matrix products, dot(): lax.dot_general(a, b, (((da,), (db,)), ((), ())), precision=precision, pr...  8.66 us
  transfers between devices with their start and end apart: 2, of which 2 were waited for; matrix products, arithmetic and copies ran while one was open for 0% of the time, Pallas kernels for 64%

profile of v3, /device:TPU:0, one launch (start us, length us, event | category | flops | bytes accessed | tf_op | source)
XLA Modules:
  0.0 141.7 jit_solution(718139043330325975)
XLA Ops:
  7.2 0.0 all-gather.2.cloned.1.call-start
  7.2 0.7 all-gather.2.cloned.1.call-update
  7.9 0.0 reduce-scatter.2.cloned.1.call-start
  7.9 0.0 copy-start.1
  8.0 1.2 copy-done.1
  9.2 0.0 copy-start.2
  9.2 1.1 copy-done.2
  10.3 0.0 copy-start.4
  10.3 1.0 copy-done.4
  11.3 80.4 %compress.1 = (f32[2048,128]{1,0:T(8,128)S(1)}, bf16[2560,256]{1,0:T(8,128)(2,1)S(1)}, bf16[128,2048]{1,0:T(8,128)(2,1)S(1)}) custom-call(bf16[2560,2048]{1,0:T(8,128)(2,1)} %bitcast.4, bf16[128,2560]{1,0:T(8,128)(2,1)S(1)} %copy-done.2, bf16[128,2048]{1,0:T(8,128)(2,1)S(1)} %copy-done.4, bf16[128,2048]{1,0:T(8,128)(2,1)S(1)} %copy-done.4, ...), custom_call_target="tpu_custom_call" | custom-call | flops 42949672960 | bytes 251658240 | tf_op jit(solution)/shard_map/compress/pallas_call | solution.py:297
  91.7 0.0 copy-start.6
  91.7 1.0 copy-done.6
  92.7 0.3 all-gather.2.cloned.1.call-done
  93.0 8.7 %fusion = f32[128,2560]{1,0:T(8,128)} fusion(bf16[128,2048]{1,0:T(8,128)(2,1)S(1)} %get-tuple-element.9, bf16[2560,2048]{1,0:T(8,128)(2,1)} %all-gather.2.cloned.1.call-done), kind=kOutput, calls=%fused_computation | convolution fusion | flops 1342177280 | bytes 12320768 | tf_op jit(solution)/shard_map/dot_general | solution.py:24
  101.7 0.0 reduce-scatter.2.cloned.1.call-update
  101.7 0.0 copy-done.3
  101.7 0.0 copy-done.5
  101.7 0.0 copy-start
  101.7 4.0 %copy-done = bf16[1,2560,2048]{2,1,0:T(8,128)(2,1)S(1)} copy-done((bf16[1,2560,2048]{2,1,0:T(8,128)(2,1)S(1)}, bf16[1,2560,2048]{2,1,0:T(8,128)(2,1)}, u32[]{:S(2)}) %copy-start) | copy-done | bytes 10485784
  105.7 1.4 %copy-done.7 = bf16[2560,256]{1,0:T(8,128)(2,1)S(1)} copy-done((bf16[2560,256]{1,0:T(8,128)(2,1)S(1)}, bf16[2560,256]{1,0:T(8,128)(2,1)}, u32[]{:S(2)}) %copy-start.7) | copy-done | bytes 1310744
  107.1 10.5 %residual.1 = (bf16[2560,2048]{1,0:T(8,128)(2,1)}, f32[320,2048]{1,0:T(8,128)}) custom-call(bf16[2560,2048]{1,0:T(8,128)(2,1)S(1)} %bitcast.5, bf16[128,2560]{1,0:T(8,128)(2,1)S(1)} %copy-done.3, bf16[128,2048]{1,0:T(8,128)(2,1)S(1)} %copy-done.5, f32[2048,128]{1,0:T(8,128)S(1)} %get-tuple-element.21.qn_ref, bf16[2560,256]{1,0:T(8,128)(2,1)S(1)} %copy-done.7), custom_call_target="tpu_custom_call" | custom-call | flops 5368709120 | bytes 20971520 | tf_op jit(solution)/shard_map/residual/pallas_call | solution.py:337
  117.7 14.6 %reduce-scatter.2.cloned.1.call-done = f32[128,640]{1,0:T(8,128)} async-done(((f32[128,2560]{1,0:T(8,128)}), f32[128,640]{1,0:T(8,128)}) %reduce-scatter.2.cloned.1.call-update) | async-done | bytes 327696 | tf_op jit(solution)/shard_map/reduce_scatter | solution.py:334
  132.2 1.7 %convert_element_type.3 = bf16[128,640]{1,0:T(8,128)(2,1)} convert(f32[128,640]{1,0:T(8,128)} %reduce-scatter.2.cloned.1.call-done) | non-fusion elementwise | flops 81920 | bytes 491520 | tf_op jit(solution)/shard_map/convert_element_type | solution.py:334
  133.9 1.0 copy.10
  (3 shorter events, 0.0 us)
Async XLA Ops:
  7.2 85.9 %all-gather.2.cloned.1.call-start = ((), (), s32[]{:S(2)}) async-start(), calls=%async_computation.1 | async-start | bytes 11796480 | tf_op jit(solution)/shard_map/all_gather | solution.py:289
  7.9 124.4 %reduce-scatter.2.cloned.1.call-start = ((), (), s32[]{:S(2)}) async-start(), calls=%async_computation.2 | async-start | bytes 1638400 | tf_op jit(solution)/shard_map/reduce_scatter | solution.py:334
  7.9 1.2 copy-start.1
  9.2 1.1 copy-start.2
  10.3 1.0 copy-start.4
  91.7 1.1 copy-start.6
  92.7 9.0 %copy-start.3 = (bf16[128,2560]{1,0:T(8,128)(2,1)S(1)}, bf16[128,2560]{1,0:T(8,128)(2,1)}, u32[]{:S(2)}) copy-start(bf16[128,2560]{1,0:T(8,128)(2,1)} %a_ref.3) | copy-start | bytes 1966084
  92.7 9.0 %copy-start.5 = (bf16[128,2048]{1,0:T(8,128)(2,1)S(1)}, bf16[128,2048]{1,0:T(8,128)(2,1)}, u32[]{:S(2)}) copy-start(bf16[128,2048]{1,0:T(8,128)(2,1)} %h_ref.3) | copy-start | bytes 1572868
  101.7 4.0 %copy-start = (bf16[1,2560,2048]{2,1,0:T(8,128)(2,1)S(1)}, bf16[1,2560,2048]{2,1,0:T(8,128)(2,1)}, u32[]{:S(2)}) copy-start(bf16[1,2560,2048]{2,1,0:T(8,128)(2,1)} %param.8) | copy-start | bytes 31457284
  105.7 1.4 %copy-start.7 = (bf16[2560,256]{1,0:T(8,128)(2,1)S(1)}, bf16[2560,256]{1,0:T(8,128)(2,1)}, u32[]{:S(2)}) copy-start(bf16[2560,256]{1,0:T(8,128)(2,1)} %copy-done.6) | copy-start | bytes 3932164
Sparse Core Ops, SparseCore 0:
  9.9 83.1 all-gather.1
  101.8 30.3 reduce-scatter.1
